TPU v7x, 32 devices: a whole 2x2x4 slice. The times are simulated.
32 devices in a mesh: dp: 8 (over z, x), tensor: 4 (over y, core).
Axes of the slice: x: 2, y: 2, z: 4, core: 2. Of those that a mesh axis runs over, the one named last changes fastest.
Arguments:
- tokens: bfloat16 [4096, 768], P(('dp', 'tensor')), may hold values from -20 to 20
- condition: bfloat16 [16, 768], P('dp'), may hold values from -4 to 4
- adaptive_weight: bfloat16 [768, 6, 768], P('dp', None, 'tensor'), may hold values from -0.21875 to 0.21875
- adaptive_bias: float32 [6, 768], P(None, 'tensor'), may hold values from -3 to 3
- entry_weight: bfloat16 [768, 3, 768], P('dp', None, 'tensor'), may hold values from -1 to 1
- entry_bias: float32 [2, 768], P(None, 'tensor'), may hold values from -3 to 3
- output_weight: bfloat16 [768, 768], P('tensor', 'dp'), may hold values from -0.875 to 0.875
- output_bias: float32 [768], replicated, may hold values from -3 to 3
- expand_weight: bfloat16 [768, 3072], P('dp', 'tensor'), may hold values from -0.21875 to 0.21875
- expand_bias: float32 [3072], P('tensor'), may hold values from -3 to 3
- reduce_weight: bfloat16 [3072, 768], P('tensor', 'dp'), may hold values from -0.109375 to 0.109375
- reduce_bias: float32 [768], replicated, may hold values from -3 to 3
- cotangent: bfloat16 [4096, 768], P(('dp', 'tensor')), may hold values from -6 to 6
Outputs:
- block_output: bfloat16 [4096, 768], P(('dp', 'tensor'))
- tokens_gradient: float32 [4096, 768], P(('dp', 'tensor'))
- condition_gradient: float32 [16, 768], P('dp')
- adaptive_gradient: float32 [768, 6, 768], P('dp', None, 'tensor')
- bias_adaptive: float32 [6, 768], P(None, 'tensor')
- entry_gradient: float32 [768, 3, 768], P('dp', None, 'tensor')
- bias_entry: float32 [2, 768], P(None, 'tensor')
- output_gradient: float32 [768, 768], P('tensor', 'dp')
- bias_output: float32 [768], replicated
- expand_gradient: float32 [768, 3072], P('dp', 'tensor')
- bias_expand: float32 [3072], P('tensor')
- reduce_gradient: float32 [3072, 768], P('tensor', 'dp')
- bias_reduce: float32 [768], replicated
All inputs are finite; a program needn't handle non-finite values.
Results may differ from a plain program's by a relative error of at most 0.015.
The roundings to bfloat16 on the way count: a program that leaves them out, or rounds other values in their place, can miss the bound.
Values may be sent and summed in bfloat16 or wider, within the bound.
A program may use at most 128 MiB of HBM per device.

v0:
```python
import jax
import jax.numpy as jnp
from jax import lax
from jax.sharding import PartitionSpec as P

HEAD_DIM = 64
LEN = 256
NORM_EPSILON = 1e-06
GELU_ROOT = 0.7978845608028654
GELU_CUBIC = 0.044715
HIGHEST_PRECISION = lax.Precision.HIGHEST


def norm_rows(values):
    center = values - jnp.mean(values, axis=-1, keepdims=True)
    inverse = lax.rsqrt(jnp.mean(center * center, axis=-1, keepdims=True) + NORM_EPSILON)
    return (center * inverse, inverse)


def norm_back(upstream, normed, inverse):
    return inverse * (
        upstream
        - jnp.mean(upstream, axis=-1, keepdims=True)
        - normed * jnp.mean(upstream * normed, axis=-1, keepdims=True)
    )


def gelu_pair(inputs):
    tangent = jnp.tanh(GELU_ROOT * (inputs + GELU_CUBIC * inputs * inputs * inputs))
    output = 0.5 * inputs * (1.0 + tangent)
    slope_value = 0.5 * (1.0 + tangent) + 0.5 * inputs * (1.0 - tangent * tangent) * GELU_ROOT * (
        1.0 + 3.0 * GELU_CUBIC * inputs * inputs
    )
    return (output, slope_value)


def contract_first(left, right):
    return lax.dot_general(
        left, right, (((0,), (0,)), ((), ())), preferred_element_type=jnp.float32
    )


def contract_last(left, right):
    return lax.dot_general(
        left, right, (((1,), (1,)), ((), ())), preferred_element_type=jnp.float32
    )


def gather_rows(values):
    return lax.all_gather(values, "tensor", axis=0, tiled=True)


def sum_rows(values):
    return lax.psum_scatter(
        values.astype(jnp.bfloat16), "tensor", scatter_dimension=0, tiled=True
    ).astype(jnp.float32)


def attend(query_rows, key_rows, value_rows):
    factor = query_rows.shape[-1] ** (-0.5)
    scores = (
        jnp.einsum("blhe,bmhe->bhlm", query_rows, key_rows, preferred_element_type=jnp.float32)
        * factor
    )
    row_top = jnp.max(scores, axis=-1, keepdims=True)
    log_total = row_top + jnp.log(jnp.sum(jnp.exp(scores - row_top), axis=-1, keepdims=True))
    weights = jnp.exp(scores - log_total).astype(jnp.bfloat16)
    attended = jnp.einsum(
        "bhlm,bmhe->blhe", weights, value_rows, preferred_element_type=jnp.float32
    )
    return (attended.astype(jnp.bfloat16), log_total)


def attend_back(query_rows, key_rows, value_rows, log_total, attended_grad):
    factor = query_rows.shape[-1] ** (-0.5)
    scores = (
        jnp.einsum("blhe,bmhe->bhlm", query_rows, key_rows, preferred_element_type=jnp.float32)
        * factor
    )
    probability = jnp.exp(scores - log_total)
    weights = probability.astype(jnp.bfloat16)
    value_grad = jnp.einsum(
        "bhlm,blhe->bmhe", weights, attended_grad, preferred_element_type=jnp.float32
    )
    weight_grad = jnp.einsum(
        "blhe,bmhe->bhlm", attended_grad, value_rows, preferred_element_type=jnp.float32
    )
    row_inner = jnp.sum(probability * weight_grad, axis=-1, keepdims=True)
    score_grad = (probability * (weight_grad - row_inner) * factor).astype(jnp.bfloat16)
    query_grad = jnp.einsum(
        "bhlm,bmhe->blhe", score_grad, key_rows, preferred_element_type=jnp.float32
    )
    key_grad = jnp.einsum(
        "bhlm,blhe->bmhe", score_grad, query_rows, preferred_element_type=jnp.float32
    )
    return (query_grad, key_grad, value_grad)


def body(
    tokens,
    condition,
    adaptive_weight,
    adaptive_bias,
    entry_weight,
    entry_bias,
    output_weight,
    output_bias,
    expand_weight,
    expand_bias,
    reduce_weight,
    reduce_bias,
    cotangent,
):
    tensor_index = lax.axis_index("tensor")
    tensor_count = lax.axis_size("tensor")
    row_count = tokens.shape[0]
    features = tokens.shape[1]
    seq_count = condition.shape[0]
    local_width = adaptive_bias.shape[1]
    local_hidden = expand_bias.shape[0]
    group_rows = row_count * tensor_count
    head_count = local_width // HEAD_DIM
    head_shape = (seq_count, LEN, head_count, HEAD_DIM)
    adaptive_full, entry_full, output_full, expand_full, reduce_full = (
        lax.all_gather(adaptive_weight, "dp", axis=0, tiled=True),
        lax.all_gather(entry_weight, "dp", axis=0, tiled=True),
        lax.all_gather(output_weight, "dp", axis=1, tiled=True),
        lax.all_gather(expand_weight, "dp", axis=0, tiled=True),
        lax.all_gather(reduce_weight, "dp", axis=1, tiled=True),
    )
    condition_float = condition.astype(jnp.float32)
    soft_condition = jax.nn.silu(condition_float).astype(jnp.bfloat16)
    modulation_local = (
        jnp.dot(
            soft_condition,
            adaptive_full.reshape(features, 6 * local_width),
            preferred_element_type=jnp.float32,
        ).reshape(seq_count, 6, local_width)
        + adaptive_bias[None]
    )
    modulation = lax.all_gather(modulation_local, "tensor", axis=2, tiled=True)
    seq_of_row = (tensor_index * row_count + jnp.arange(row_count, dtype=jnp.int32)) // LEN
    selector = (seq_of_row[:, None] == jnp.arange(seq_count, dtype=jnp.int32)[None, :]).astype(
        jnp.float32
    )
    per_row = jnp.dot(
        selector, modulation.reshape(seq_count, 6 * features), precision=HIGHEST_PRECISION
    ).reshape(row_count, 6, features)
    shift_one, scale_one, gate_one, shift_two, scale_two, gate_two = [
        per_row[:, column] for column in range(6)
    ]
    inputs = tokens.astype(jnp.float32)
    normed_one, inverse_one = norm_rows(inputs)
    attention_local = (normed_one * (1.0 + scale_one) + shift_one).astype(jnp.bfloat16)
    attention_input = gather_rows(attention_local)
    projected = jnp.dot(
        attention_input,
        entry_full.reshape(features, 3 * local_width),
        preferred_element_type=jnp.float32,
    ).reshape(group_rows, 3, local_width)
    query_rows = (projected[:, 0] + entry_bias[0]).astype(jnp.bfloat16).reshape(head_shape)
    key_rows = projected[:, 1].astype(jnp.bfloat16).reshape(head_shape)
    value_rows = (projected[:, 2] + entry_bias[1]).astype(jnp.bfloat16).reshape(head_shape)
    attended, log_total = attend(query_rows, key_rows, value_rows)
    attended = attended.reshape(group_rows, local_width)
    attention_branch = (
        sum_rows(jnp.dot(attended, output_full, preferred_element_type=jnp.float32)) + output_bias
    )
    middle = inputs + gate_one * attention_branch
    normed_two, inverse_two = norm_rows(middle)
    feed_local = (normed_two * (1.0 + scale_two) + shift_two).astype(jnp.bfloat16)
    feed_input = gather_rows(feed_local)
    hidden_pre = jnp.dot(feed_input, expand_full, preferred_element_type=jnp.float32) + expand_bias
    hidden_value, hidden_slope = gelu_pair(hidden_pre)
    hidden_rows = hidden_value.astype(jnp.bfloat16)
    feed_branch = (
        sum_rows(jnp.dot(hidden_rows, reduce_full, preferred_element_type=jnp.float32))
        + reduce_bias
    )
    block_output = (middle + gate_two * feed_branch).astype(jnp.bfloat16)
    adaptive_back, entry_back, output_back, expand_back, reduce_back = (
        lax.all_gather(adaptive_weight, "dp", axis=0, tiled=True),
        lax.all_gather(entry_weight, "dp", axis=0, tiled=True),
        lax.all_gather(output_weight, "dp", axis=1, tiled=True),
        lax.all_gather(expand_weight, "dp", axis=0, tiled=True),
        lax.all_gather(reduce_weight, "dp", axis=1, tiled=True),
    )
    upstream = cotangent.astype(jnp.float32)
    feed_grad = upstream * gate_two
    feed_gathered = gather_rows(feed_grad.astype(jnp.bfloat16))
    reduce_total = contract_first(hidden_rows, feed_gathered)
    hidden_grad = contract_last(feed_gathered, reduce_back) * hidden_slope
    hidden_round = hidden_grad.astype(jnp.bfloat16)
    expand_total = contract_first(feed_input, hidden_round)
    feed_input_grad = sum_rows(contract_last(hidden_round, expand_back))
    middle_grad = upstream + norm_back(feed_input_grad * (1.0 + scale_two), normed_two, inverse_two)
    attention_grad = middle_grad * gate_one
    attention_gathered = gather_rows(attention_grad.astype(jnp.bfloat16))
    output_total = contract_first(attended, attention_gathered)
    attended_grad = (
        contract_last(attention_gathered, output_back).astype(jnp.bfloat16).reshape(head_shape)
    )
    query_grad, key_grad, value_grad = attend_back(
        query_rows, key_rows, value_rows, log_total, attended_grad
    )
    query_grad = query_grad.reshape(group_rows, local_width)
    key_grad = key_grad.reshape(group_rows, local_width)
    value_grad = value_grad.reshape(group_rows, local_width)
    entry_round = (
        jnp.stack([query_grad, key_grad, value_grad], axis=1)
        .astype(jnp.bfloat16)
        .reshape(group_rows, 3 * local_width)
    )
    entry_total = contract_first(attention_input, entry_round).reshape(features, 3, local_width)
    input_grad = sum_rows(contract_last(entry_round, entry_back.reshape(features, 3 * local_width)))
    tokens_gradient = middle_grad + norm_back(
        input_grad * (1.0 + scale_one), normed_one, inverse_one
    )
    row_terms = jnp.stack(
        [
            input_grad,
            input_grad * normed_one,
            middle_grad * attention_branch,
            feed_input_grad,
            feed_input_grad * normed_two,
            upstream * feed_branch,
        ],
        axis=1,
    )
    per_sequence = lax.dot_general(
        selector,
        row_terms.reshape(row_count, 6 * features),
        (((0,), (0,)), ((), ())),
        precision=HIGHEST_PRECISION,
        preferred_element_type=jnp.float32,
    ).reshape(seq_count, 6, features)
    modulation_grad = lax.psum_scatter(
        per_sequence.astype(jnp.bfloat16), "tensor", scatter_dimension=2, tiled=True
    ).astype(jnp.float32)
    modulation_round = modulation_grad.astype(jnp.bfloat16).reshape(seq_count, 6 * local_width)
    adaptive_total = contract_first(soft_condition, modulation_round).reshape(
        features, 6, local_width
    )
    condition_partial = contract_last(
        modulation_round, adaptive_back.reshape(features, 6 * local_width)
    )
    condition_sum = lax.psum(condition_partial, "tensor")
    sigmoid_value = jax.nn.sigmoid(condition_float)
    condition_gradient = (
        condition_sum * sigmoid_value * (1.0 + condition_float * (1.0 - sigmoid_value))
    )
    adaptive_gradient, entry_gradient, output_gradient, expand_gradient, reduce_gradient = (
        lax.psum_scatter(adaptive_total, "dp", scatter_dimension=0, tiled=True),
        lax.psum_scatter(entry_total, "dp", scatter_dimension=0, tiled=True),
        lax.psum_scatter(output_total, "dp", scatter_dimension=1, tiled=True),
        lax.psum_scatter(expand_total, "dp", scatter_dimension=0, tiled=True),
        lax.psum_scatter(reduce_total, "dp", scatter_dimension=1, tiled=True),
    )
    width_start = tensor_index * local_width
    hidden_start = tensor_index * local_hidden
    adaptive_slot = lax.dynamic_update_slice_in_dim(
        jnp.zeros((6, features), jnp.float32), jnp.sum(modulation_grad, axis=0), width_start, 1
    )
    entry_slot = lax.dynamic_update_slice_in_dim(
        jnp.zeros((2, features), jnp.float32),
        jnp.stack([jnp.sum(query_grad, axis=0), jnp.sum(value_grad, axis=0)]),
        width_start,
        1,
    )
    expand_slot = lax.dynamic_update_slice_in_dim(
        jnp.zeros((local_hidden * tensor_count,), jnp.float32),
        jnp.sum(hidden_grad, axis=0),
        hidden_start,
        0,
    )
    adaptive_sums, entry_sums, output_sums, expand_sums, reduce_sums = lax.psum(
        (
            adaptive_slot,
            entry_slot,
            jnp.sum(attention_grad, axis=0),
            expand_slot,
            jnp.sum(feed_grad, axis=0),
        ),
        ("dp", "tensor"),
    )
    bias_adaptive = lax.dynamic_slice_in_dim(adaptive_sums, width_start, local_width, 1)
    bias_entry = lax.dynamic_slice_in_dim(entry_sums, width_start, local_width, 1)
    bias_expand = lax.dynamic_slice_in_dim(expand_sums, hidden_start, local_hidden, 0)
    return (
        block_output,
        tokens_gradient,
        condition_gradient,
        adaptive_gradient,
        bias_adaptive,
        entry_gradient,
        bias_entry,
        output_gradient,
        output_sums,
        expand_gradient,
        bias_expand,
        reduce_gradient,
        reduce_sums,
    )


def solution(mesh):
    in_specs = (
        P(("dp", "tensor"), None),
        P("dp", None),
        P("dp", None, "tensor"),
        P(None, "tensor"),
        P("dp", None, "tensor"),
        P(None, "tensor"),
        P("tensor", "dp"),
        P(),
        P("dp", "tensor"),
        P("tensor"),
        P("tensor", "dp"),
        P(),
        P(("dp", "tensor"), None),
    )
    out_specs = (
        P(("dp", "tensor"), None),
        P(("dp", "tensor"), None),
        P("dp", None),
        P("dp", None, "tensor"),
        P(None, "tensor"),
        P("dp", None, "tensor"),
        P(None, "tensor"),
        P("tensor", "dp"),
        P(),
        P("dp", "tensor"),
        P("tensor"),
        P("tensor", "dp"),
        P(),
    )
    return jax.shard_map(body, mesh=mesh, in_specs=in_specs, out_specs=out_specs, check_vma=False)
```

profile of v0, /device:TPU:0, one launch (start us, length us, event | category | flops | bytes accessed | tf_op | source)
XLA Modules:
  0.0 773.9 jit_solution(14435792287438220595)
XLA Ops:
  8.0 39.2 %all_gather.38 = bf16[768,3,192]{2,0,1:T(8,128)(2,1)S(1)} all-gather(bf16[96,3,192]{2,0,1:T(8,128)(2,1)} %param.17), channel_id=1, replica_groups=mesh['dp'=8,'tensor'=4] {'dp'}, dimensions={0}, use_global_device_ids=true | all-gather | bytes 995328 | tf_op jit(solution)/shard_map/all_gather | solution.py:126
  48.5 34.3 %all_gather.39 = bf16[192,768]{0,1:T(8,128)(2,1)} all-gather(bf16[192,96]{0,1:T(8,128)(2,1)S(1)} %copy.88), channel_id=1, replica_groups=mesh['dp'=8,'tensor'=4] {'dp'}, dimensions={1}, use_global_device_ids=true | all-gather | bytes 331776 | tf_op jit(solution)/shard_map/all_gather | solution.py:127
  82.9 2.8 copy.79
  86.4 8.9 %all_gather.36 = f32[2,6,768]{1,0,2:T(2,128)S(1)} all-gather(f32[2,6,192]{1,0,2:T(2,128)S(1)} %copy.80), channel_id=1, replica_groups=mesh['dp'=8,'tensor'=4] {'tensor'}, dimensions={2}, use_global_device_ids=true | all-gather | bytes 46080 | tf_op jit(solution)/shard_map/all_gather | solution.py:141
  97.1 8.7 %all_gather.37 = bf16[512,768]{1,0:T(8,128)(2,1)S(1)} all-gather(bf16[128,768]{1,0:T(8,128)(2,1)S(1)} %fusion.52), channel_id=1, replica_groups=mesh['dp'=8,'tensor'=4] {'tensor'}, dimensions={0}, use_global_device_ids=true | all-gather | bytes 983040 | tf_op jit(solution)/shard_map/all_gather | solution.py:50
  112.6 1.9 fusion.26
  118.2 20.9 %reduce-scatter.15.cloned.1.call-done = bf16[128,768]{1,0:T(8,128)(2,1)} async-done(((bf16[512,768]{1,0:T(8,128)(2,1)}), bf16[128,768]{1,0:T(8,128)(2,1)}) %reduce-scatter.15.cloned.1.call-update) | async-done | bytes 196624 | tf_op jit(solution)/shard_map/reduce_scatter | solution.py:54
  140.6 8.5 %all_gather.40 = bf16[512,768]{1,0:T(8,128)(2,1)} all-gather(bf16[128,768]{1,0:T(8,128)(2,1)S(1)} %get-tuple-element.34), channel_id=1, replica_groups=mesh['dp'=8,'tensor'=4] {'tensor'}, dimensions={0}, use_global_device_ids=true | all-gather | bytes 983040 | tf_op jit(solution)/shard_map/all_gather | solution.py:50
  149.0 9.1 %all_gather.43 = bf16[512,768]{1,0:T(8,128)(2,1)} all-gather(bf16[128,768]{1,0:T(8,128)(2,1)S(1)} %get-tuple-element.33), channel_id=1, replica_groups=mesh['dp'=8,'tensor'=4] {'tensor'}, dimensions={0}, use_global_device_ids=true | all-gather | bytes 983040 | tf_op jit(solution)/shard_map/all_gather | solution.py:50
  158.2 24.2 %all-gather.6.cloned.1.call-done = bf16[768,768]{1,0:T(8,128)(2,1)} async-done(((bf16[96,768]{1,0:T(8,128)(2,1)}), bf16[768,768]{1,0:T(8,128)(2,1)}) %all-gather.6.cloned.1.call-update) | async-done | bytes 1179664 | tf_op jit(solution)/shard_map/all_gather | solution.py:128
  182.4 3.5 convolution_add_fusion
  185.9 38.4 %all-gather.8.cloned.1.call-done = bf16[768,768]{0,1:T(8,128)(2,1)} async-done(((bf16[768,96]{0,1:T(8,128)(2,1)}), bf16[768,768]{0,1:T(8,128)(2,1)}) %all-gather.8.cloned.1.call-update) | async-done | bytes 1179664 | tf_op jit(solution)/shard_map/all_gather | solution.py:129
  224.3 4.1 fusion.123
  231.1 3.8 convolution_convert_fusion.1
  234.9 18.2 %reduce-scatter.19.cloned.1.call-done = bf16[128,768]{1,0:T(8,128)(2,1)} async-done(((bf16[512,768]{1,0:T(8,128)(2,1)}), bf16[128,768]{1,0:T(8,128)(2,1)}) %reduce-scatter.19.cloned.1.call-update) | async-done | bytes 196624 | tf_op jit(solution)/shard_map/reduce_scatter | solution.py:54
  254.7 24.0 %reduce-scatter.17.cloned.1.call-done = bf16[128,768]{1,0:T(8,128)(2,1)} async-done(((bf16[512,768]{1,0:T(8,128)(2,1)}), bf16[128,768]{1,0:T(8,128)(2,1)}) %reduce-scatter.17.cloned.1.call-update) | async-done | bytes 196624 | tf_op jit(solution)/shard_map/reduce_scatter | solution.py:54
  278.7 2.0 fusion.86
  280.7 8.2 %all_gather.44 = bf16[512,768]{1,0:T(8,128)(2,1)S(1)} all-gather(bf16[128,768]{1,0:T(8,128)(2,1)S(1)} %get-tuple-element.28), channel_id=1, replica_groups=mesh['dp'=8,'tensor'=4] {'tensor'}, dimensions={0}, use_global_device_ids=true | all-gather | bytes 983040 | tf_op jit(solution)/shard_map/all_gather | solution.py:50
  291.8 2.6 fusion.81
  294.5 4.9 fusion.120
  299.4 4.4 fusion.23
  303.9 3.1 fusion.119
  307.8 1.7 stack_reshape.9
  309.6 1.8 copy.94
  311.4 1.7 stack_reshape.10
  315.1 3.3 bitcast_convert_fusion
  318.5 23.8 %reduce-scatter.21.cloned.1.call-done = bf16[128,768]{1,0:T(8,128)(2,1)} async-done(((bf16[512,768]{1,0:T(8,128)(2,1)}), bf16[128,768]{1,0:T(8,128)(2,1)}) %reduce-scatter.21.cloned.1.call-update) | async-done | bytes 196624 | tf_op jit(solution)/shard_map/reduce_scatter | solution.py:54
  342.3 1.7 fusion.63
  344.0 1.9 fusion.65
  345.9 1.7 bitcast_dynamic-update-slice_fusion
  350.9 3.1 copy.98
  353.9 3.4 fusion.27
  357.3 2.7 copy.108
  360.0 2.7 reshape.177
  364.3 3.6 fusion.72
  369.1 3.8 fusion.115
  374.1 3.4 fusion.36
  377.7 5.0 reduce-scatter.31.cloned.1.call-done
  384.2 3.0 fusion.99
  394.1 55.1 %reduce-scatter.33.cloned.1.call-done = f32[96,192]{1,0:T(8,128)} async-done(((f32[768,192]{1,0:T(8,128)}), f32[96,192]{1,0:T(8,128)}) %reduce-scatter.33.cloned.1.call-update) | async-done | bytes 73744
  450.8 1.7 fusion.76
  454.8 42.1 %all-reduce = (f32[6,768]{1,0:T(8,128)S(1)}, f32[2,768]{1,0:T(2,128)S(1)}, f32[768]{0:T(1024)}, f32[3072]{0:T(1024)S(1)}, f32[768]{0:T(1024)}) all-reduce(f32[6,768]{1,0:T(8,128)S(1)} %dynamic_update_slice.9, f32[2,768]{1,0:T(2,128)} %dynamic_update_slice.10, ...), channel_id=1, replica_groups=mesh['dp'=8,'tensor'=4] {'dp','tensor'}, use_global_device_ids=true, to_apply=%region_19.20 | all-reduce | flops 10752 | bytes 86016 | tf_op jit(solution)/shard_map/psum | solution.py:276
  497.6 2.4 convolution_bitcast_fusion.2
  499.9 5.9 psum.42
  507.7 14.8 %reduce-scatter.27.cloned.1.call-done = f32[96,768]{1,0:T(8,128)} async-done(((f32[768,768]{1,0:T(8,128)}), f32[96,768]{1,0:T(8,128)}) %reduce-scatter.27.cloned.1.call-update) | async-done | bytes 294928 | tf_op jit(solution)/shard_map/reduce_scatter | solution.py:256
  522.6 72.9 %reduce-scatter.29.cloned.1.call-done = f32[768,96]{0,1:T(8,128)} async-done(((f32[768,768]{0,1:T(8,128)}), f32[768,96]{0,1:T(8,128)}) %reduce-scatter.29.cloned.1.call-update) | async-done | bytes 294928 | tf_op jit(solution)/shard_map/reduce_scatter | solution.py:257
  595.5 72.7 %reduce-scatter.25.cloned.1.call-done = f32[96,3,192]{2,0,1:T(8,128)} async-done(((f32[768,3,192]{2,0,1:T(8,128)}), f32[96,3,192]{2,0,1:T(8,128)}) %reduce-scatter.25.cloned.1.call-update) | async-done | bytes 221200 | tf_op jit(solution)/shard_map/reduce_scatter | solution.py:254
  668.2 99.1 %reduce-scatter.23.cloned.1.call-done = f32[96,6,192]{2,0,1:T(8,128)} async-done(((f32[768,6,192]{2,0,1:T(8,128)}), f32[96,6,192]{2,0,1:T(8,128)}) %reduce-scatter.23.cloned.1.call-update) | async-done | bytes 442384 | tf_op jit(solution)/shard_map/reduce_scatter | solution.py:253
  (186 shorter events, 48.6 us)
Async XLA Ops:
  7.2 75.7 %all-gather.4.cloned.1.call-start = ((), (), s32[]{:S(2)}) async-start(), calls=%async_computation.10 | async-start | bytes 2654208 | tf_op jit(solution)/shard_map/all_gather | solution.py:125
  7.9 131.2 %reduce-scatter.15.cloned.1.call-start = ((), (), s32[]{:S(2)}) async-start(), calls=%async_computation.11 | async-start | bytes 983040 | tf_op jit(solution)/shard_map/reduce_scatter | solution.py:54
  8.0 39.9 %copy-start.42 = (f32[2,192]{1,0:T(2,128)S(1)}, f32[2,192]{1,0:T(2,128)}, u32[]{:S(2)}) copy-start(f32[2,192]{1,0:T(2,128)} %param.18) | copy-start | bytes 4612
  8.0 40.1 %copy-start.27 = (bf16[192,96]{1,0:T(8,128)(2,1)S(1)}, bf16[192,96]{1,0:T(8,128)(2,1)}, u32[]{:S(2)}) copy-start(bf16[192,96]{1,0:T(8,128)(2,1)} %param.19) | copy-start | bytes 110596
  8.0 40.2 %copy-start.1 = (bf16[128,768]{1,0:T(8,128)(2,1)S(1)}, bf16[128,768]{1,0:T(8,128)(2,1)}, u32[]{:S(2)}) copy-start(bf16[128,768]{1,0:T(8,128)(2,1)} %param.13) | copy-start | bytes 589828
  47.2 35.6 %copy-start.6 = (bf16[768,3,192]{2,0,1:T(8,128)(2,1)}, bf16[768,3,192]{2,0,1:T(8,128)(2,1)S(1)}, u32[]{:S(2)}) copy-start(bf16[768,3,192]{2,0,1:T(8,128)(2,1)S(1)} %all_gather.38) | copy-start | bytes 2654212
  48.0 62.4 %copy-start.38 = (f32[3,64]{1,0:T(4,128)}, f32[3,64]{1,0:T(4,128)S(1)}, u32[]{:S(2)}) copy-start(f32[3,64]{1,0:T(4,128)S(1)} %add.200) | copy-start | bytes 2308
  48.2 47.6 %copy-start.43 = (s32[128]{0:T(128)}, s32[128]{0:T(128)S(1)}, u32[]{:S(2)}) copy-start(s32[128]{0:T(128)S(1)} %and_select_fusion) | copy-start | bytes 1540
  48.3 48.6 %copy-start.32 = (f32[128]{0:T(128)}, f32[128]{0:T(128)S(1)}, u32[]{:S(2)}) copy-start(f32[128]{0:T(128)S(1)} %broadcast_multiply_fusion.5) | copy-start | bytes 1540
  82.8 14.1 %copy-start.37 = (f32[128]{0:T(128)}, f32[128]{0:T(128)S(1)}, u32[]{:S(2)}) copy-start(f32[128]{0:T(128)S(1)} %add_rsqrt_fusion.1) | copy-start | bytes 1540
  109.2 3.0 copy-start.18
  112.5 4.3 copy-start.7
  112.6 2.9 copy-start.8
  114.5 24.6 %copy-start.29 = (f32[768]{0:T(1024)S(1)}, f32[768]{0:T(1024)}, u32[]{:S(2)}) copy-start(f32[768]{0:T(1024)} %param.20) | copy-start | bytes 9220
  116.8 23.5 %copy-start.14 = (bf16[128,768]{1,0:T(8,128)(2,1)S(1)}, bf16[128,768]{1,0:T(8,128)(2,1)}, u32[]{:S(2)}) copy-start(bf16[128,768]{1,0:T(8,128)(2,1)} %param.25) | copy-start | bytes 589828
  116.9 65.5 %all-gather.6.cloned.1.call-start = ((), (), s32[]{:S(2)}) async-start(), calls=%async_computation.12 | async-start | bytes 1327104 | tf_op jit(solution)/shard_map/all_gather | solution.py:128
  117.6 106.7 %all-gather.8.cloned.1.call-start = ((), (), s32[]{:S(2)}) async-start(), calls=%async_computation.13 | async-start | bytes 1327104 | tf_op jit(solution)/shard_map/all_gather | solution.py:129
  118.2 134.9 %reduce-scatter.19.cloned.1.call-start = ((), (), s32[]{:S(2)}) async-start(), calls=%async_computation.15 | async-start | bytes 983040 | tf_op jit(solution)/shard_map/reduce_scatter | solution.py:54
  140.2 8.9 %copy-start.34 = (f32[128]{0:T(128)}, f32[128]{0:T(128)S(1)}, u32[]{:S(2)}) copy-start(f32[128]{0:T(128)S(1)} %broadcast_multiply_fusion.4) | copy-start | bytes 1540
  140.4 8.7 %copy-start.40 = (f32[128]{0:T(128)}, f32[128]{0:T(128)S(1)}, u32[]{:S(2)}) copy-start(f32[128]{0:T(128)S(1)} %add_rsqrt_fusion) | copy-start | bytes 1540
  224.3 5.0 copy-start.45
  231.0 22.1 %copy-start.35 = (f32[128]{0:T(128)S(1)}, f32[128]{0:T(128)}, u32[]{:S(2)}) copy-start(f32[128]{0:T(128)} %copy-done.34) | copy-start | bytes 1540
  231.0 22.1 %copy-start.41 = (f32[128]{0:T(128)S(1)}, f32[128]{0:T(128)}, u32[]{:S(2)}) copy-start(f32[128]{0:T(128)} %copy-done.40) | copy-start | bytes 1540
  231.0 47.7 %reduce-scatter.17.cloned.1.call-start = ((), (), s32[]{:S(2)}) async-start(), calls=%async_computation.14 | async-start | bytes 983040 | tf_op jit(solution)/shard_map/reduce_scatter | solution.py:54
  234.9 107.4 %reduce-scatter.21.cloned.1.call-start = ((), (), s32[]{:S(2)}) async-start(), calls=%async_computation.16 | async-start | bytes 983040 | tf_op jit(solution)/shard_map/reduce_scatter | solution.py:54
  278.7 11.1 %copy-start.9 = (bf16[192,768]{0,1:T(8,128)(2,1)S(1)}, bf16[192,768]{0,1:T(8,128)(2,1)}, u32[]{:S(2)}) copy-start(bf16[192,768]{0,1:T(8,128)(2,1)} %all_gather.39) | copy-start | bytes 884740
  280.7 65.3 %copy-start.4 = (f32[128,768]{1,0:T(8,128)}, f32[128,768]{1,0:T(8,128)S(1)}, u32[]{:S(2)}) copy-start(f32[128,768]{1,0:T(8,128)S(1)} %get-tuple-element.29) | copy-start | bytes 1179652
  294.5 5.0 copy-start.39
  303.9 3.1 copy-start.26
  306.9 6.2 copy-start.20
  315.0 3.4 copy-start.25
  315.1 29.0 %copy-start.33 = (f32[128]{0:T(128)S(1)}, f32[128]{0:T(128)}, u32[]{:S(2)}) copy-start(f32[128]{0:T(128)} %copy-done.32) | copy-start | bytes 1540
  318.4 27.5 %copy-start.30 = (f32[768]{0:T(1024)S(1)}, f32[768]{0:T(1024)}, u32[]{:S(2)}) copy-start(f32[768]{0:T(1024)} %param.20) | copy-start | bytes 9220
  318.4 29.3 %copy-start.13 = (bf16[128,768]{1,0:T(8,128)(2,1)S(1)}, bf16[128,768]{1,0:T(8,128)(2,1)}, u32[]{:S(2)}) copy-start(bf16[128,768]{1,0:T(8,128)(2,1)} %reduce-scatter.19.cloned.1.call-done) | copy-start | bytes 589828
  318.4 64.3 %reduce-scatter.31.cloned.1.call-start = ((), (), s32[]{:S(2)}) async-start(), calls=%async_computation.21 | async-start | bytes 245760
  344.0 6.0 copy-start.15
  344.0 6.0 copy-start.21
  344.0 6.0 copy-start.31
  350.9 3.1 copy-start.44
  357.3 5.5 copy-start.3
  357.3 5.5 copy-start.17
  362.8 86.4 %reduce-scatter.33.cloned.1.call-start = ((), (), s32[]{:S(2)}) async-start(), calls=%async_computation.22 | async-start | bytes 884736
  364.2 158.3 %reduce-scatter.27.cloned.1.call-start = ((), (), s32[]{:S(2)}) async-start(), calls=%async_computation.19 | async-start | bytes 2654208 | tf_op jit(solution)/shard_map/reduce_scatter | solution.py:256
  368.0 227.5 %reduce-scatter.29.cloned.1.call-start = ((), (), s32[]{:S(2)}) async-start(), calls=%async_computation.20 | async-start | bytes 2654208 | tf_op jit(solution)/shard_map/reduce_scatter | solution.py:257
  372.9 295.3 %reduce-scatter.25.cloned.1.call-start = ((), (), s32[]{:S(2)}) async-start(), calls=%async_computation.18 | async-start | bytes 2654208 | tf_op jit(solution)/shard_map/reduce_scatter | solution.py:254
  377.4 389.9 %reduce-scatter.23.cloned.1.call-start = ((), (), s32[]{:S(2)}) async-start(), calls=%async_computation.17 | async-start | bytes 5308416 | tf_op jit(solution)/shard_map/reduce_scatter | solution.py:253
  387.2 63.6 %copy-start.5 = (f32[128,768]{1,0:T(8,128)S(1)}, f32[128,768]{1,0:T(8,128)}, u32[]{:S(2)}) copy-start(f32[128,768]{1,0:T(8,128)} %copy-done.4) | copy-start | bytes 1179652
  387.2 63.6 %copy-start.10 = (bf16[128,768]{1,0:T(8,128)(2,1)S(1)}, bf16[128,768]{1,0:T(8,128)(2,1)}, u32[]{:S(2)}) copy-start(bf16[128,768]{1,0:T(8,128)(2,1)} %reduce-scatter.21.cloned.1.call-done) | copy-start | bytes 589828
  (11 other events, 16.2 us)
Sparse Core Ops, SparseCore 0:
  10.2 65.9 all-gather.3
  117.0 22.0 reduce-scatter.14
  141.3 41.0 all-gather.5
  184.4 39.8 all-gather.7
  231.1 21.9 reduce-scatter.18
  255.5 23.1 reduce-scatter.16
  318.5 23.7 reduce-scatter.20
  362.9 19.7 reduce-scatter.30
  386.0 63.1 reduce-scatter.32
  453.1 69.3 reduce-scatter.26
  526.6 68.8 reduce-scatter.28
  599.4 68.7 reduce-scatter.24
  672.4 94.8 reduce-scatter.22
where the time goes:
time: 775 us; the launch traced here: 774 us
  waiting for transfers between devices  471 us (61%)
  blocking collectives  165 us (21%)
  matrix products  59.7 us (8%)
  local copies, waits for them, and re-layouts  43.4 us (6%)
  other arithmetic  19.6 us (3%)
  between operations  14.4 us (2%)
    reduce_scatter x1, waiting for transfers between devices, body(): lax.psum_scatter(adaptive_total, 'dp', scatter_dimension=0, tiled=True)  99.1 us
    reduce_scatter x4, waiting for transfers between devices, sum_rows(): lax.psum_scatter(values.astype(jnp.bfloat16), 'tensor', scatter_dimension...  86.8 us
    reduce_scatter x1, waiting for transfers between devices, body(): lax.psum_scatter(reduce_total, 'dp', scatter_dimension=1, tiled=True)  72.9 us
    reduce_scatter x1, waiting for transfers between devices, body(): lax.psum_scatter(entry_total, 'dp', scatter_dimension=0, tiled=True)  72.7 us
    unnamed x15, waiting for transfers between devices  62.1 us
    psum x1, blocking collectives, body(): lax.psum((adaptive_slot, entry_slot, jnp.sum(attention_grad, axis=0), exp...  42.1 us
    all_gather x1, blocking collectives, body(): lax.all_gather(entry_weight, 'dp', axis=0, tiled=True)  39.2 us
    all_gather x1, waiting for transfers between devices, body(): lax.all_gather(reduce_weight, 'dp', axis=1, tiled=True)  38.4 us
  transfers between devices with their start and end apart: 13, of which 12 were waited for; matrix products, arithmetic and copies ran while one was open for 6% of the time, Pallas kernels for 0%

commit v1 on v0

--- a/solution.py
+++ b/solution.py
@@ -9,6 +9,35 @@
 GELU_ROOT = 0.7978845608028654
 GELU_CUBIC = 0.044715
 HIGHEST_PRECISION = lax.Precision.HIGHEST
+
+
+def step_on_node_by_axis(xx, out_dim):
+    xx = jnp.moveaxis(xx, 0, out_dim)
+    val2 = xx.shape
+    return xx.reshape(*val2[:out_dim], val2[out_dim] * val2[out_dim + 1], *val2[out_dim + 2 :])
+
+
+def step_on_ports(view, mesh_name):
+    u_next = jax.lax.axis_size(mesh_name)
+    arr_now = jax.lax.axis_index(mesh_name)
+    t1, taken_in = (u_next, arr_now)
+    mat_out, tile_out = (view[None], 1)
+    while tile_out < t1:
+        sides = []
+        for c in [*range(t1)]:
+            sides.append((c, c ^ tile_out))
+        frame_out = jax.lax.ppermute(mat_out, mesh_name, sides)
+        value_now = taken_in & tile_out == 0
+        b_next = jnp.where(value_now, mat_out, frame_out)
+        low = jnp.where(value_now, frame_out, mat_out)
+        mat_out = jnp.concatenate([b_next, low])
+        tile_out *= 2
+    return mat_out
+
+
+def runs_apply(page, piece_in, dim_i):
+    kept_arr = step_on_ports(page, piece_in)
+    return step_on_node_by_axis(kept_arr, dim_i)
 
 
 def norm_rows(values):
@@ -123,7 +152,7 @@
     head_shape = (seq_count, LEN, head_count, HEAD_DIM)
     adaptive_full, entry_full, output_full, expand_full, reduce_full = (
         lax.all_gather(adaptive_weight, "dp", axis=0, tiled=True),
-        lax.all_gather(entry_weight, "dp", axis=0, tiled=True),
+        runs_apply(entry_weight, "dp", 0),
         lax.all_gather(output_weight, "dp", axis=1, tiled=True),
         lax.all_gather(expand_weight, "dp", axis=0, tiled=True),
         lax.all_gather(reduce_weight, "dp", axis=1, tiled=True),

time: 775 us -> 787 us (1.015)
  waiting for transfers between devices: 471 us -> 445 us
  blocking collectives: 165 us -> 189 us
  starting transfers between devices: 0.75 us -> 10.6 us
    reduce_scatter x4, waiting for transfers between devices: 86.8 us -> 48.6 us  [sum_rows(): lax.psum_scatter(values.astype(jnp.bfloat16), 'tensor', scatter_dimension...]
    all_gather x1, blocking collectives: 34.3 us -> 61.9 us  [body(): lax.all_gather(output_weight, 'dp', axis=1, tiled=True)]
    ppermute x0 -> x3, waiting for transfers between devices: none -> 11.9 us  [step_on_ports(): frame_out = jax.lax.ppermute(mat_out, mesh_name, sides)]
    ppermute x0 -> x3, starting transfers between devices: none -> 9.87 us  [step_on_ports(): frame_out = jax.lax.ppermute(mat_out, mesh_name, sides)]
  transfers between devices with their start and end apart: 13 -> 16, of which waited for: 12 -> 13; matrix products, arithmetic and copies ran while one was open for 6% -> 6% of each run, Pallas kernels for 0% -> 0%
where the time goes in v1:
time: 787 us; the launch traced here: 785 us
  waiting for transfers between devices  445 us (57%)
  blocking collectives  189 us (24%)
  matrix products  59.7 us (8%)
  local copies, waits for them, and re-layouts  45.1 us (6%)
  other arithmetic  22 us (3%)
  between operations  14.5 us (2%)
  starting transfers between devices  10.6 us (1%)
    reduce_scatter x1, waiting for transfers between devices, body(): lax.psum_scatter(adaptive_total, 'dp', scatter_dimension=0, tiled=True)  99.1 us
    reduce_scatter x1, waiting for transfers between devices, body(): lax.psum_scatter(reduce_total, 'dp', scatter_dimension=1, tiled=True)  72.9 us
    reduce_scatter x1, waiting for transfers between devices, body(): lax.psum_scatter(entry_total, 'dp', scatter_dimension=0, tiled=True)  72.8 us
    unnamed x15, waiting for transfers between devices  62.3 us
    all_gather x1, blocking collectives, body(): lax.all_gather(output_weight, 'dp', axis=1, tiled=True)  61.9 us
    reduce_scatter x4, waiting for transfers between devices, sum_rows(): lax.psum_scatter(values.astype(jnp.bfloat16), 'tensor', scatter_dimension...  48.6 us
    psum x1, blocking collectives, body(): lax.psum((adaptive_slot, entry_slot, jnp.sum(attention_grad, axis=0), exp...  42.3 us
    all_gather x1, waiting for transfers between devices, body(): lax.all_gather(reduce_weight, 'dp', axis=1, tiled=True)  38.4 us
  transfers between devices with their start and end apart: 16, of which 13 were waited for; matrix products, arithmetic and copies ran while one was open for 6% of the time, Pallas kernels for 0%

profile of v1, /device:TPU:0, one launch (start us, length us, event | category | flops | bytes accessed | tf_op | source)
XLA Modules:
  0.0 785.4 jit_solution(12139653998249942037)
XLA Ops:
  8.0 3.0 collective-permute-start
  12.1 3.0 collective-permute-done
  16.1 1.9 collective-permute-start.1
  18.5 8.9 %collective-permute-done.1 = bf16[2,96,3,192]{3,1,2,0:T(8,128)(2,1)S(1)} collective-permute-done((bf16[2,96,3,192]{3,1,2,0:T(8,128)(2,1)S(1)}, bf16[2,96,3,192]{3,1,2,0:T(8,128)(2,1)S(1)}, u32[]{:S(2)}, u32[]{:S(2)}) %collective-permute-start.1) | collective-permute-done | bytes 221216 | tf_op jit(solution)/shard_map/ppermute | solution.py:29
  27.5 5.0 collective-permute-start.2
  32.5 61.9 %all_gather.37 = bf16[192,768]{0,1:T(8,128)(2,1)} all-gather(bf16[192,96]{0,1:T(8,128)(2,1)S(1)} %copy.88), channel_id=1, replica_groups=mesh['dp'=8,'tensor'=4] {'dp'}, dimensions={1}, use_global_device_ids=true | all-gather | bytes 331776 | tf_op jit(solution)/shard_map/all_gather | solution.py:156
  97.2 2.8 copy.79
  100.8 8.7 %all_gather.35 = f32[2,6,768]{1,0,2:T(2,128)S(1)} all-gather(f32[2,6,192]{1,0,2:T(2,128)S(1)} %copy.80), channel_id=1, replica_groups=mesh['dp'=8,'tensor'=4] {'tensor'}, dimensions={2}, use_global_device_ids=true | all-gather | bytes 46080 | tf_op jit(solution)/shard_map/all_gather | solution.py:170
  111.3 8.7 %all_gather.36 = bf16[512,768]{1,0:T(8,128)(2,1)S(1)} all-gather(bf16[128,768]{1,0:T(8,128)(2,1)S(1)} %fusion.51), channel_id=1, replica_groups=mesh['dp'=8,'tensor'=4] {'tensor'}, dimensions={0}, use_global_device_ids=true | all-gather | bytes 983040 | tf_op jit(solution)/shard_map/all_gather | solution.py:79
  126.7 1.9 fusion.26
  132.3 18.3 %reduce-scatter.15.cloned.1.call-done = bf16[128,768]{1,0:T(8,128)(2,1)} async-done(((bf16[512,768]{1,0:T(8,128)(2,1)}), bf16[128,768]{1,0:T(8,128)(2,1)}) %reduce-scatter.15.cloned.1.call-update) | async-done | bytes 196624 | tf_op jit(solution)/shard_map/reduce_scatter | solution.py:83
  152.1 8.5 %all_gather.38 = bf16[512,768]{1,0:T(8,128)(2,1)} all-gather(bf16[128,768]{1,0:T(8,128)(2,1)S(1)} %get-tuple-element.34), channel_id=1, replica_groups=mesh['dp'=8,'tensor'=4] {'tensor'}, dimensions={0}, use_global_device_ids=true | all-gather | bytes 983040 | tf_op jit(solution)/shard_map/all_gather | solution.py:79
  160.6 9.3 %all_gather.41 = bf16[512,768]{1,0:T(8,128)(2,1)} all-gather(bf16[128,768]{1,0:T(8,128)(2,1)S(1)} %get-tuple-element.33), channel_id=1, replica_groups=mesh['dp'=8,'tensor'=4] {'tensor'}, dimensions={0}, use_global_device_ids=true | all-gather | bytes 983040 | tf_op jit(solution)/shard_map/all_gather | solution.py:79
  169.9 24.0 %all-gather.6.cloned.1.call-done = bf16[768,768]{1,0:T(8,128)(2,1)} async-done(((bf16[96,768]{1,0:T(8,128)(2,1)}), bf16[768,768]{1,0:T(8,128)(2,1)}) %all-gather.6.cloned.1.call-update) | async-done | bytes 1179664 | tf_op jit(solution)/shard_map/all_gather | solution.py:157
  193.9 3.5 convolution_add_fusion
  197.4 38.4 %all-gather.8.cloned.1.call-done = bf16[768,768]{0,1:T(8,128)(2,1)} async-done(((bf16[768,96]{0,1:T(8,128)(2,1)}), bf16[768,768]{0,1:T(8,128)(2,1)}) %all-gather.8.cloned.1.call-update) | async-done | bytes 1179664 | tf_op jit(solution)/shard_map/all_gather | solution.py:158
  235.8 4.1 fusion.122
  242.6 3.8 convolution_convert_fusion.1
  246.5 35.4 %all_gather.43 = bf16[768,3,192]{2,0,1:T(8,128)(2,1)} all-gather(bf16[96,3,192]{2,0,1:T(8,128)(2,1)S(1)} %copy-done.23), channel_id=1, replica_groups=mesh['dp'=8,'tensor'=4] {'dp'}, dimensions={0}, use_global_device_ids=true | all-gather | bytes 995328 | tf_op jit(solution)/shard_map/all_gather | solution.py:212
  283.6 6.7 reduce-scatter.17.cloned.1.call-done
  290.2 2.0 fusion.85
  292.2 8.0 %all_gather.42 = bf16[512,768]{1,0:T(8,128)(2,1)S(1)} all-gather(bf16[128,768]{1,0:T(8,128)(2,1)S(1)} %get-tuple-element.28), channel_id=1, replica_groups=mesh['dp'=8,'tensor'=4] {'tensor'}, dimensions={0}, use_global_device_ids=true | all-gather | bytes 983040 | tf_op jit(solution)/shard_map/all_gather | solution.py:79
  303.2 2.6 fusion.80
  305.8 5.0 fusion.119
  310.8 4.4 fusion.23
  315.2 3.1 fusion.118
  319.2 1.7 stack_reshape.9
  320.9 1.8 copy.94
  326.4 3.4 bitcast_convert_fusion
  330.1 23.6 %reduce-scatter.21.cloned.1.call-done = bf16[128,768]{1,0:T(8,128)(2,1)} async-done(((bf16[512,768]{1,0:T(8,128)(2,1)}), bf16[128,768]{1,0:T(8,128)(2,1)}) %reduce-scatter.21.cloned.1.call-update) | async-done | bytes 196624 | tf_op jit(solution)/shard_map/reduce_scatter | solution.py:83
  355.4 1.9 fusion.64
  362.3 3.1 copy.98
  365.3 3.4 fusion.27
  368.8 2.7 copy.108
  371.4 2.7 reshape.173
  375.7 3.7 fusion.71
  380.5 3.8 fusion.114
  385.5 3.3 fusion.34
  388.9 5.2 reduce-scatter.31.cloned.1.call-done
  395.6 3.0 fusion.98
  405.6 55.0 %reduce-scatter.33.cloned.1.call-done = f32[96,192]{1,0:T(8,128)} async-done(((f32[768,192]{1,0:T(8,128)}), f32[96,192]{1,0:T(8,128)}) %reduce-scatter.33.cloned.1.call-update) | async-done | bytes 73744
  466.1 42.3 %all-reduce = (f32[6,768]{1,0:T(8,128)S(1)}, f32[2,768]{1,0:T(2,128)S(1)}, f32[768]{0:T(1024)}, f32[3072]{0:T(1024)S(1)}, f32[768]{0:T(1024)}) all-reduce(f32[6,768]{1,0:T(8,128)S(1)} %dynamic_update_slice.9, f32[2,768]{1,0:T(2,128)} %dynamic_update_slice.10, ...), channel_id=1, replica_groups=mesh['dp'=8,'tensor'=4] {'dp','tensor'}, use_global_device_ids=true, to_apply=%region_19.20 | all-reduce | flops 10752 | bytes 86016 | tf_op jit(solution)/shard_map/psum | solution.py:305
  509.1 2.4 convolution_bitcast_fusion.2
  511.4 5.9 psum.42
  519.3 14.8 %reduce-scatter.27.cloned.1.call-done = f32[96,768]{1,0:T(8,128)} async-done(((f32[768,768]{1,0:T(8,128)}), f32[96,768]{1,0:T(8,128)}) %reduce-scatter.27.cloned.1.call-update) | async-done | bytes 294928 | tf_op jit(solution)/shard_map/reduce_scatter | solution.py:285
  534.0 72.9 %reduce-scatter.29.cloned.1.call-done = f32[768,96]{0,1:T(8,128)} async-done(((f32[768,768]{0,1:T(8,128)}), f32[768,96]{0,1:T(8,128)}) %reduce-scatter.29.cloned.1.call-update) | async-done | bytes 294928 | tf_op jit(solution)/shard_map/reduce_scatter | solution.py:286
  606.9 72.8 %reduce-scatter.25.cloned.1.call-done = f32[96,3,192]{2,0,1:T(8,128)} async-done(((f32[768,3,192]{2,0,1:T(8,128)}), f32[96,3,192]{2,0,1:T(8,128)}) %reduce-scatter.25.cloned.1.call-update) | async-done | bytes 221200 | tf_op jit(solution)/shard_map/reduce_scatter | solution.py:283
  679.7 99.1 %reduce-scatter.23.cloned.1.call-done = f32[96,6,192]{2,0,1:T(8,128)} async-done(((f32[768,6,192]{2,0,1:T(8,128)}), f32[96,6,192]{2,0,1:T(8,128)}) %reduce-scatter.23.cloned.1.call-update) | async-done | bytes 442384 | tf_op jit(solution)/shard_map/reduce_scatter | solution.py:282
  (199 shorter events, 59.5 us)
Async XLA Ops:
  7.2 11.1 %copy-start.1 = (bf16[128,768]{1,0:T(8,128)(2,1)S(1)}, bf16[128,768]{1,0:T(8,128)(2,1)}, u32[]{:S(2)}) copy-start(bf16[128,768]{1,0:T(8,128)(2,1)} %param.13) | copy-start | bytes 589828
  7.2 10.8 %copy-start.42 = (f32[2,192]{1,0:T(2,128)S(1)}, f32[2,192]{1,0:T(2,128)}, u32[]{:S(2)}) copy-start(f32[2,192]{1,0:T(2,128)} %param.18) | copy-start | bytes 4612
  7.2 11.0 %copy-start.27 = (bf16[192,96]{1,0:T(8,128)(2,1)S(1)}, bf16[192,96]{1,0:T(8,128)(2,1)}, u32[]{:S(2)}) copy-start(bf16[192,96]{1,0:T(8,128)(2,1)} %param.19) | copy-start | bytes 110596
  7.2 90.0 %all-gather.4.cloned.1.call-start = ((), (), s32[]{:S(2)}) async-start(), calls=%async_computation.10 | async-start | bytes 2654208 | tf_op jit(solution)/shard_map/all_gather | solution.py:154
  7.9 142.6 %reduce-scatter.15.cloned.1.call-start = ((), (), s32[]{:S(2)}) async-start(), calls=%async_computation.11 | async-start | bytes 983040 | tf_op jit(solution)/shard_map/reduce_scatter | solution.py:83
  8.0 7.1 collective-permute-start
  12.1 99.0 %copy-start.32 = (f32[128]{0:T(128)}, f32[128]{0:T(128)S(1)}, u32[]{:S(2)}) copy-start(f32[128]{0:T(128)S(1)} %broadcast_multiply_fusion.5) | copy-start | bytes 1540
  16.1 11.3 %collective-permute-start.1 = (bf16[2,96,3,192]{3,1,2,0:T(8,128)(2,1)S(1)}, bf16[2,96,3,192]{3,1,2,0:T(8,128)(2,1)S(1)}, u32[]{:S(2)}, u32[]{:S(2)}) collective-permute-start(bf16[2,96,3,192]{3,1,2,0:T(8,128)(2,1)S(1)} %pad_maximum_fusion.2), channel_id=1, source_target_pairs={{0,8},{4,12},{8,0},{12,4},{16,24},{20,28},{24,16},{28,20},{1,9},{5... | collective-permute-start | bytes 663560 | tf_op jit(solution)/shard_map/ppermute | solution.py:29
  18.1 106.4 %copy-start.38 = (f32[3,64]{1,0:T(4,128)}, f32[3,64]{1,0:T(4,128)S(1)}, u32[]{:S(2)}) copy-start(f32[3,64]{1,0:T(4,128)S(1)} %add.200) | copy-start | bytes 2308
  27.5 66.9 %collective-permute-start.2 = (bf16[4,96,3,192]{3,1,2,0:T(8,128)(2,1)S(1)}, bf16[4,96,3,192]{3,1,2,0:T(8,128)(2,1)S(1)}, u32[]{:S(2)}, u32[]{:S(2)}) collective-permute-start(bf16[4,96,3,192]{3,1,2,0:T(8,128)(2,1)S(1)} %pad_maximum_fusion.1), channel_id=1, source_target_pairs={{0,16},{4,20},{8,24},{12,28},{16,0},{20,4},{24,8},{28,12},{1,17},{... | collective-permute-start | bytes 1327112 | tf_op jit(solution)/shard_map/ppermute | solution.py:29
  32.5 77.4 %copy-start.43 = (s32[128]{0:T(128)}, s32[128]{0:T(128)S(1)}, u32[]{:S(2)}) copy-start(s32[128]{0:T(128)S(1)} %and_select_fusion) | copy-start | bytes 1540
  94.4 16.6 %copy-start.37 = (f32[128]{0:T(128)}, f32[128]{0:T(128)S(1)}, u32[]{:S(2)}) copy-start(f32[128]{0:T(128)S(1)} %add_rsqrt_fusion.1) | copy-start | bytes 1540
  126.7 4.2 copy-start.6
  128.6 22.0 %copy-start.29 = (f32[768]{0:T(1024)S(1)}, f32[768]{0:T(1024)}, u32[]{:S(2)}) copy-start(f32[768]{0:T(1024)} %param.20) | copy-start | bytes 9220
  130.9 21.0 %copy-start.13 = (bf16[128,768]{1,0:T(8,128)(2,1)S(1)}, bf16[128,768]{1,0:T(8,128)(2,1)}, u32[]{:S(2)}) copy-start(bf16[128,768]{1,0:T(8,128)(2,1)} %param.25) | copy-start | bytes 589828
  130.9 63.0 %all-gather.6.cloned.1.call-start = ((), (), s32[]{:S(2)}) async-start(), calls=%async_computation.12 | async-start | bytes 1327104 | tf_op jit(solution)/shard_map/all_gather | solution.py:157
  131.6 104.2 %all-gather.8.cloned.1.call-start = ((), (), s32[]{:S(2)}) async-start(), calls=%async_computation.13 | async-start | bytes 1327104 | tf_op jit(solution)/shard_map/all_gather | solution.py:158
  132.2 149.7 %reduce-scatter.19.cloned.1.call-start = ((), (), s32[]{:S(2)}) async-start(), calls=%async_computation.15 | async-start | bytes 983040 | tf_op jit(solution)/shard_map/reduce_scatter | solution.py:83
  151.7 8.9 %copy-start.34 = (f32[128]{0:T(128)}, f32[128]{0:T(128)S(1)}, u32[]{:S(2)}) copy-start(f32[128]{0:T(128)S(1)} %broadcast_multiply_fusion.4) | copy-start | bytes 1540
  151.9 8.7 %copy-start.40 = (f32[128]{0:T(128)}, f32[128]{0:T(128)S(1)}, u32[]{:S(2)}) copy-start(f32[128]{0:T(128)S(1)} %add_rsqrt_fusion) | copy-start | bytes 1540
  235.8 5.0 copy-start.45
  242.5 4.0 copy-start.23
  242.5 47.7 %reduce-scatter.17.cloned.1.call-start = ((), (), s32[]{:S(2)}) async-start(), calls=%async_computation.14 | async-start | bytes 983040 | tf_op jit(solution)/shard_map/reduce_scatter | solution.py:83
  246.4 35.5 %copy-start.35 = (f32[128]{0:T(128)S(1)}, f32[128]{0:T(128)}, u32[]{:S(2)}) copy-start(f32[128]{0:T(128)} %copy-done.34) | copy-start | bytes 1540
  246.4 35.5 %copy-start.41 = (f32[128]{0:T(128)S(1)}, f32[128]{0:T(128)}, u32[]{:S(2)}) copy-start(f32[128]{0:T(128)} %copy-done.40) | copy-start | bytes 1540
  246.4 107.3 %reduce-scatter.21.cloned.1.call-start = ((), (), s32[]{:S(2)}) async-start(), calls=%async_computation.16 | async-start | bytes 983040 | tf_op jit(solution)/shard_map/reduce_scatter | solution.py:83
  290.2 10.9 %copy-start.8 = (bf16[192,768]{0,1:T(8,128)(2,1)S(1)}, bf16[192,768]{0,1:T(8,128)(2,1)}, u32[]{:S(2)}) copy-start(bf16[192,768]{0,1:T(8,128)(2,1)} %all_gather.37) | copy-start | bytes 884740
  292.2 65.1 %copy-start.4 = (f32[128,768]{1,0:T(8,128)}, f32[128,768]{1,0:T(8,128)S(1)}, u32[]{:S(2)}) copy-start(f32[128,768]{1,0:T(8,128)S(1)} %get-tuple-element.29) | copy-start | bytes 1179652
  305.8 5.0 copy-start.39
  318.3 6.2 copy-start.19
  326.4 3.4 copy-start.25
  326.4 29.0 %copy-start.33 = (f32[128]{0:T(128)S(1)}, f32[128]{0:T(128)}, u32[]{:S(2)}) copy-start(f32[128]{0:T(128)} %copy-done.32) | copy-start | bytes 1540
  329.8 27.6 %copy-start.30 = (f32[768]{0:T(1024)S(1)}, f32[768]{0:T(1024)}, u32[]{:S(2)}) copy-start(f32[768]{0:T(1024)} %param.20) | copy-start | bytes 9220
  329.8 29.3 %copy-start.12 = (bf16[128,768]{1,0:T(8,128)(2,1)S(1)}, bf16[128,768]{1,0:T(8,128)(2,1)}, u32[]{:S(2)}) copy-start(bf16[128,768]{1,0:T(8,128)(2,1)} %reduce-scatter.19.cloned.1.call-done) | copy-start | bytes 589828
  329.8 64.3 %reduce-scatter.31.cloned.1.call-start = ((), (), s32[]{:S(2)}) async-start(), calls=%async_computation.21 | async-start | bytes 245760
  355.4 6.0 copy-start.14
  355.4 6.0 copy-start.20
  355.4 6.0 copy-start.31
  362.3 3.1 copy-start.44
  368.8 5.5 copy-start.3
  368.8 5.5 copy-start.16
  374.2 86.4 %reduce-scatter.33.cloned.1.call-start = ((), (), s32[]{:S(2)}) async-start(), calls=%async_computation.22 | async-start | bytes 884736
  375.7 158.4 %reduce-scatter.27.cloned.1.call-start = ((), (), s32[]{:S(2)}) async-start(), calls=%async_computation.19 | async-start | bytes 2654208 | tf_op jit(solution)/shard_map/reduce_scatter | solution.py:285
  379.4 227.5 %reduce-scatter.29.cloned.1.call-start = ((), (), s32[]{:S(2)}) async-start(), calls=%async_computation.20 | async-start | bytes 2654208 | tf_op jit(solution)/shard_map/reduce_scatter | solution.py:286
  384.4 295.4 %reduce-scatter.25.cloned.1.call-start = ((), (), s32[]{:S(2)}) async-start(), calls=%async_computation.18 | async-start | bytes 2654208 | tf_op jit(solution)/shard_map/reduce_scatter | solution.py:283
  388.8 390.0 %reduce-scatter.23.cloned.1.call-start = ((), (), s32[]{:S(2)}) async-start(), calls=%async_computation.17 | async-start | bytes 5308416 | tf_op jit(solution)/shard_map/reduce_scatter | solution.py:282
  398.6 63.6 %copy-start.5 = (f32[128,768]{1,0:T(8,128)S(1)}, f32[128,768]{1,0:T(8,128)}, u32[]{:S(2)}) copy-start(f32[128,768]{1,0:T(8,128)} %copy-done.4) | copy-start | bytes 1179652
  398.6 63.6 %copy-start.9 = (bf16[128,768]{1,0:T(8,128)(2,1)S(1)}, bf16[128,768]{1,0:T(8,128)(2,1)}, u32[]{:S(2)}) copy-start(bf16[128,768]{1,0:T(8,128)(2,1)} %reduce-scatter.21.cloned.1.call-done) | copy-start | bytes 589828
  (14 other events, 25.0 us)
Sparse Core Ops, SparseCore 0:
  10.2 72.7 all-gather.3
  131.0 19.5 reduce-scatter.14
  152.8 41.0 all-gather.5
  196.0 39.8 all-gather.7
  242.7 21.8 reduce-scatter.18
  267.0 23.2 reduce-scatter.16
  329.9 23.7 reduce-scatter.20
  374.3 19.7 reduce-scatter.30
  397.4 63.1 reduce-scatter.32
  464.5 69.4 reduce-scatter.26
  538.1 68.7 reduce-scatter.28
  610.8 68.8 reduce-scatter.24
  683.9 94.8 reduce-scatter.22
